TPU v7x, 128 devices: a whole 4x4x4 slice. The times are simulated.
128 devices in a mesh: row: 8 (over z, core), col: 16 (over x, y).
Axes of the slice: x: 4, y: 4, z: 4, core: 2. Of those that a mesh axis runs over, the one named last changes fastest.
Arguments:
- left_edge: bfloat16 [16, 3072, 3072], P('row', 'col'), may hold values from -6 to 6
- right_edge: bfloat16 [16, 3072, 3072], P('row', 'col'), may hold values from -0.109375 to 0.109375
- projector: bfloat16 [16, 3072, 64], P('row'), may hold values from -0.109375 to 0.109375
- sector_size: int32 [16], P('row'), may hold values from 1 to 3072, 30720 in all
Outputs:
- enlarged: float32 [16, 3072, 3072], P('row', 'col')
- new_corner: float32 [16, 64, 64], P('row')
All inputs are finite; a program needn't handle non-finite values. No bound on the sum of `sector_size` on one device may be relied on, other than what follows from the above.
Results may differ from a plain program's by a relative error of at most 0.0003.
Values may be sent and summed in bfloat16 or wider, within the bound.
No kernel may reach another device: no remote copies, remote signals or barrier semaphores. Data moves between devices by JAX's collectives and lax.ppermute only.
A program may use at most 128 MiB of HBM per device.

v0:
```python
import jax
import jax.numpy as jnp
from jax import lax
from jax.sharding import PartitionSpec as P


def body(left_edge, right_edge, projector, sector_size):
    count = left_edge.shape[0]
    rows = left_edge.shape[1]
    width = projector.shape[1]
    kept = projector.shape[2]
    first_row = lax.axis_index("col") * rows
    states = jnp.arange(width, dtype=jnp.int32)
    live = (states[None, :] < sector_size[:, None]).astype(jnp.bfloat16)
    masked = projector * live[:, :, None]
    own_masked = lax.dynamic_slice_in_dim(masked, first_row, rows, 1).astype(jnp.float32)
    enlarged = jnp.einsum(
        "sik,skj->sij",
        left_edge,
        lax.all_gather(right_edge, "col", axis=1, tiled=True),
        preferred_element_type=jnp.float32,
    )
    inner = jnp.einsum(
        "sij,sjq->siq", enlarged, masked.astype(jnp.float32), precision=lax.Precision.HIGHEST
    )
    parts = jnp.einsum("sip,siq->spq", own_masked, inner, precision=lax.Precision.HIGHEST)
    entries = lax.axis_size("row") * count * kept * kept
    corner = lax.psum(parts, "col")
    total = lax.psum(jnp.sum(corner * corner), "row")
    return (enlarged, corner * lax.rsqrt(total / entries + 1e-06))


def solution(mesh):
    placed = (P("row", "col", None), P("row", "col", None), P("row", None, None), P("row"))
    return jax.shard_map(
        body,
        mesh=mesh,
        in_specs=placed,
        out_specs=(P("row", "col", None), P("row", None, None)),
        check_vma=False,
    )
```

profile of v0, /device:TPU:1, one launch (start us, length us, event | category | flops | bytes accessed | tf_op | source)
XLA Modules:
  0.0 348.4 jit_solution(8765672397625688852)
XLA Ops:
  7.2 0.0 copy-start
  7.2 0.0 all-gather.2.cloned.1.call-start
  7.2 0.7 all-gather.2.cloned.1.call-update
  7.9 0.7 compare_convert_fusion
  8.7 1.2 broadcast_multiply_fusion
  9.9 221.9 %all-gather.2.cloned.1.call-done = bf16[2,3072,3072]{2,1,0:T(8,128)(2,1)} async-done(((bf16[2,192,3072]{2,1,0:T(8,128)(2,1)}), bf16[2,3072,3072]{2,1,0:T(8,128)(2,1)}) %all-gather.2.cloned.1.call-update) | async-done | bytes 37748752 | tf_op jit(solution)/shard_map/all_gather | solution.py:20
  231.8 0.0 copy-done
  231.8 16.9 %fusion.3 = f32[2,192,3072]{2,1,0:T(8,128)} fusion(bf16[2,192,3072]{2,1,0:T(8,128)(2,1)S(1)} %copy-done, bf16[2,3072,3072]{2,1,0:T(8,128)(2,1)} %all-gather.2.cloned.1.call-done), kind=kOutput, calls=%fused_computation.7 | convolution fusion | flops 7247757312 | bytes 44826624 | tf_op jit(solution)/shard_map/sik,skj->sij/dot_general | solution.py:17
  248.6 5.0 %fusion.4 = f32[2,192,64]{1,2,0:T(8,128)S(1)} fusion(f32[2,192,3072]{2,1,0:T(8,128)} %fusion.3, bf16[2,3072,64]{1,2,0:T(8,128)(2,1)S(1)} %broadcast_multiply_fusion), kind=kOutput, calls=%fused_computation.8 | convolution fusion | flops 905969664 | bytes 5603328 | tf_op jit(solution)/shard_map/sij,sjq->siq/dot_general | solution.py:23
  253.6 0.3 fusion
  253.9 58.6 %psum.14 = f32[2,64,64]{2,1,0:T(8,128)S(1)} all-reduce(f32[2,64,64]{2,1,0:T(8,128)S(1)} %fusion), channel_id=1, replica_groups=mesh['row'=8,'col'=16] {'col'}, use_global_device_ids=true, to_apply=%region_0.0 | all-reduce | flops 8192 | bytes 65536 | tf_op jit(solution)/shard_map/psum | solution.py:28
  312.5 0.6 multiply_reduce_fusion
  313.1 27.0 %psum.15 = f32[]{:T(128)} all-reduce(f32[]{:T(128)} %multiply_reduce_fusion), channel_id=1, replica_groups=mesh['row'=8,'col'=16] {'row'}, use_global_device_ids=true, to_apply=%region_2.0 | all-reduce | flops 1 | bytes 8 | tf_op jit(solution)/shard_map/psum | solution.py:29
  340.9 0.6 broadcast_multiply_fusion.1
Async XLA Ops:
  7.2 224.6 %copy-start = (bf16[2,192,3072]{2,1,0:T(8,128)(2,1)S(1)}, bf16[2,192,3072]{2,1,0:T(8,128)(2,1)}, u32[]{:S(2)}) copy-start(bf16[2,192,3072]{2,1,0:T(8,128)(2,1)} %param.4) | copy-start | bytes 7077892
  7.2 224.6 %all-gather.2.cloned.1.call-start = ((), (), s32[]{:S(2)}) async-start(), calls=%async_computation | async-start | bytes 40108032 | tf_op jit(solution)/shard_map/all_gather | solution.py:20
Sparse Core Ops, SparseCore 0:
  10.2 221.5 all-gather.1
where the time goes:
time: 349 us; the launch traced here: 348 us
  waiting for transfers between devices  223 us (64%)
  blocking collectives  85.7 us (25%)
  matrix products  22.1 us (6%)
  between operations  14.7 us (4%)
    all_gather x1, waiting for transfers between devices, body(): lax.all_gather(right_edge, 'col', axis=1, tiled=True)  222 us
    psum x1, blocking collectives, body(): corner = lax.psum(parts, 'col')  58.6 us
    psum x1, blocking collectives, body(): total = lax.psum(jnp.sum(corner * corner), 'row')  27 us
    dot_general x1, matrix products, body(): jnp.einsum('sik,skj->sij', left_edge, lax.all_gather(right_edge, 'col', a...  16.9 us
  transfers between devices with their start and end apart: 1, of which 1 were waited for; matrix products, arithmetic and copies ran while one was open for 1% of the time, Pallas kernels for 0%

commit v1 on v0

--- a/solution.py
+++ b/solution.py
@@ -25,7 +25,7 @@
     )
     parts = jnp.einsum("sip,siq->spq", own_masked, inner, precision=lax.Precision.HIGHEST)
     entries = lax.axis_size("row") * count * kept * kept
-    corner = lax.psum(parts, "col")
+    corner = jnp.sum(lax.all_gather(parts, "col"), axis=0)
     total = lax.psum(jnp.sum(corner * corner), "row")
     return (enlarged, corner * lax.rsqrt(total / entries + 1e-06))
 

time: 349 us -> 300 us (0.86)
  blocking collectives: 85.7 us -> 37.5 us
    psum x1 -> x0, blocking collectives: 58.6 us -> none  [body(): corner = lax.psum(parts, 'col')]
    all_gather x0 -> x1, blocking collectives: none -> 19.3 us  [body(): corner = jnp.sum(lax.all_gather(parts, 'col'), axis=0)]
    psum x1, blocking collectives: 27 us -> 18.2 us  [body(): total = lax.psum(jnp.sum(corner * corner), 'row')]
where the time goes in v1:
time: 300 us
  waiting for transfers between devices  223 us (74%)
  blocking collectives  37.5 us (12%)
  matrix products  22.1 us (7%)
  between operations  14.7 us (5%)
  other arithmetic  3.27 us (1%)
    all_gather x1, waiting for transfers between devices, body(): lax.all_gather(right_edge, 'col', axis=1, tiled=True)  222 us
    all_gather x1, blocking collectives, body(): corner = jnp.sum(lax.all_gather(parts, 'col'), axis=0)  19.3 us
    psum x1, blocking collectives, body(): total = lax.psum(jnp.sum(corner * corner), 'row')  18.2 us
    dot_general x1, matrix products, body(): jnp.einsum('sik,skj->sij', left_edge, lax.all_gather(right_edge, 'col', a...  16.9 us
  transfers between devices with their start and end apart: 1, of which 1 were waited for; matrix products, arithmetic and copies ran while one was open for 1% of the time, Pallas kernels for 0%

profile of v1, /device:TPU:1, one launch (start us, length us, event | category | flops | bytes accessed | tf_op | source)
XLA Modules:
  0.0 300.2 jit_solution(6875226940043721463)
XLA Ops:
  7.2 0.0 copy-start
  7.2 0.0 all-gather.3.cloned.1.call-start
  7.2 0.7 all-gather.3.cloned.1.call-update
  7.9 0.7 compare_convert_fusion
  8.7 1.2 broadcast_multiply_fusion
  9.9 221.9 %all-gather.3.cloned.1.call-done = bf16[2,3072,3072]{2,1,0:T(8,128)(2,1)} async-done(((bf16[2,192,3072]{2,1,0:T(8,128)(2,1)}), bf16[2,3072,3072]{2,1,0:T(8,128)(2,1)}) %all-gather.3.cloned.1.call-update) | async-done | bytes 37748752 | tf_op jit(solution)/shard_map/all_gather | solution.py:20
  231.8 0.0 copy-done
  231.8 16.9 %fusion.3 = f32[2,192,3072]{2,1,0:T(8,128)} fusion(bf16[2,192,3072]{2,1,0:T(8,128)(2,1)S(1)} %copy-done, bf16[2,3072,3072]{2,1,0:T(8,128)(2,1)} %all-gather.3.cloned.1.call-done), kind=kOutput, calls=%fused_computation.7 | convolution fusion | flops 7247757312 | bytes 44826624 | tf_op jit(solution)/shard_map/sik,skj->sij/dot_general | solution.py:17
  248.6 5.0 %fusion.4 = f32[2,192,64]{1,2,0:T(8,128)S(1)} fusion(f32[2,192,3072]{2,1,0:T(8,128)} %fusion.3, bf16[2,3072,64]{1,2,0:T(8,128)(2,1)S(1)} %broadcast_multiply_fusion), kind=kOutput, calls=%fused_computation.8 | convolution fusion | flops 905969664 | bytes 5603328 | tf_op jit(solution)/shard_map/sij,sjq->siq/dot_general | solution.py:23
  253.6 0.3 fusion
  253.9 19.3 %all-gather = f32[32,64,64]{2,1,0:T(8,128)S(1)} all-gather(f32[2,64,64]{2,1,0:T(8,128)S(1)} %fusion), channel_id=2, replica_groups=mesh['row'=8,'col'=16] {'col'}, dimensions={0}, use_global_device_ids=true | all-gather | bytes 557056 | tf_op jit(solution)/shard_map/all_gather | solution.py:28
  273.2 0.1 reduce_sum.18
  273.3 0.6 multiply_reduce_fusion
  273.9 18.2 %psum.7 = f32[]{:T(128)} all-reduce(f32[]{:T(128)} %multiply_reduce_fusion), channel_id=1, replica_groups=mesh['row'=8,'col'=16] {'row'}, use_global_device_ids=true, to_apply=%region_2.0 | all-reduce | flops 1 | bytes 8 | tf_op jit(solution)/shard_map/psum | solution.py:29
  292.8 0.6 broadcast_multiply_fusion.1
Async XLA Ops:
  7.2 224.6 %copy-start = (bf16[2,192,3072]{2,1,0:T(8,128)(2,1)S(1)}, bf16[2,192,3072]{2,1,0:T(8,128)(2,1)}, u32[]{:S(2)}) copy-start(bf16[2,192,3072]{2,1,0:T(8,128)(2,1)} %param.4) | copy-start | bytes 7077892
  7.2 224.6 %all-gather.3.cloned.1.call-start = ((), (), s32[]{:S(2)}) async-start(), calls=%async_computation | async-start | bytes 40108032 | tf_op jit(solution)/shard_map/all_gather | solution.py:20
Sparse Core Ops, SparseCore 0:
  10.2 221.5 all-gather.2

commit v2 on v0

--- a/solution.py
+++ b/solution.py
@@ -17,7 +17,9 @@
     enlarged = jnp.einsum(
         "sik,skj->sij",
         left_edge,
-        lax.all_gather(right_edge, "col", axis=1, tiled=True),
+        jnp.concatenate(
+            lax.all_to_all(jnp.stack([right_edge] * lax.axis_size("col")), "col", 0, 0), axis=1
+        ),
         preferred_element_type=jnp.float32,
     )
     inner = jnp.einsum(

time: 349 us -> 862 us (2.47)
  waiting for transfers between devices: 223 us -> 700 us
  local copies, waits for them, and re-layouts: 0.01 us -> 39.3 us
  between operations: 14.7 us -> 1.37 us
    all_to_all x0 -> x1, waiting for transfers between devices: none -> 700 us  [body(): lax.all_to_all(jnp.stack([right_edge] * lax.axis_size('col')), 'col', 0, 0)]
    all_gather x1 -> x0, waiting for transfers between devices: 222 us -> none  [body(): lax.all_gather(right_edge, 'col', axis=1, tiled=True)]
    reshape x0 -> x1, local copies, waits for them, and re-layouts: none -> 25.5 us  [body(): jnp.concatenate(lax.all_to_all(jnp.stack([right_edge] * lax.axis_size('co...]
    another operation x0 -> x1, local copies, waits for them, and re-layouts: none -> 13.8 us  [body(): jnp.stack([right_edge] * lax.axis_size('col'))]
  transfers between devices with their start and end apart: 1 -> 1, of which waited for: 1 -> 1; matrix products, arithmetic and copies ran while one was open for 1% -> 0% of each run, Pallas kernels for 0% -> 0%
where the time goes in v2:
time: 862 us
  waiting for transfers between devices  700 us (81%)
  blocking collectives  88.8 us (10%)
  local copies, waits for them, and re-layouts  39.3 us (5%)
  matrix products  22.1 us (3%)
    all_to_all x1, waiting for transfers between devices, body(): lax.all_to_all(jnp.stack([right_edge] * lax.axis_size('col')), 'col', 0, 0)  700 us
    psum x1, blocking collectives, body(): corner = lax.psum(parts, 'col')  59.5 us
    psum x1, blocking collectives, body(): total = lax.psum(jnp.sum(corner * corner), 'row')  29.3 us
    reshape x1, local copies, waits for them, and re-layouts, body(): jnp.concatenate(lax.all_to_all(jnp.stack([right_edge] * lax.axis_size('co...  25.5 us
  transfers between devices with their start and end apart: 1, of which 1 were waited for; matrix products, arithmetic and copies ran while one was open for 0% of the time, Pallas kernels for 0%

profile of v2, /device:TPU:1, one launch (start us, length us, event | category | flops | bytes accessed | tf_op | source)
XLA Modules:
  0.0 861.8 jit_solution(1789313120721175357)
XLA Ops:
  0.6 0.0 copy-start
  0.6 13.8 %stack.2 = bf16[16,2,192,3072]{3,2,1,0:T(8,128)(2,1)} broadcast(bf16[2,192,3072]{2,1,0:T(8,128)(2,1)} %param.5), dimensions={1,2,3} | broadcast | bytes 40108032 | tf_op jit(solution)/shard_map/stack | solution.py:21
  14.4 0.0 copy-start.1
  14.4 7.8 all-to-all-start
  22.2 0.0 copy-done.1
  22.2 0.1 compare_convert_fusion
  22.3 1.2 broadcast_multiply_fusion
  23.5 699.9 %all-to-all-done = bf16[16,2,192,3072]{3,2,1,0:T(8,128)(2,1)} async-done(((bf16[16,2,192,3072]{3,2,1,0:T(8,128)(2,1)}), bf16[16,2,192,3072]{3,2,1,0:T(8,128)(2,1)}, u32[]{:S(2)}, u32[]{:S(2)}) %all-to-all-start) | async-done | bytes 37748768 | tf_op jit(solution)/shard_map/all_to_all | solution.py:21
  723.4 25.5 %copy.6 = bf16[2,16,192,3072]{3,2,1,0:T(8,128)(2,1)} copy(bf16[2,16,192,3072]{3,2,0,1:T(8,128)(2,1)} %bitcast) | data formatting | bytes 75497472 | tf_op jit(solution)/shard_map/reshape | solution.py:20
  748.9 0.0 copy-done
  748.9 16.9 %fusion.3 = f32[2,192,3072]{2,1,0:T(8,128)} fusion(bf16[2,192,3072]{2,1,0:T(8,128)(2,1)S(1)} %copy-done, bf16[2,3072,3072]{2,1,0:T(8,128)(2,1)} %bitcast.7), kind=kOutput, calls=%fused_computation.7 | convolution fusion | flops 7247757312 | bytes 44826624 | tf_op jit(solution)/shard_map/sik,skj->sij/dot_general | solution.py:17
  765.8 5.0 fusion.4
  770.8 0.3 fusion
  771.0 59.5 %psum.14 = f32[2,64,64]{2,1,0:T(8,128)S(1)} all-reduce(f32[2,64,64]{2,1,0:T(8,128)S(1)} %fusion), channel_id=1, replica_groups=mesh['row'=8,'col'=16] {'col'}, use_global_device_ids=true, to_apply=%region_0.0 | all-reduce | flops 8192 | bytes 65536 | tf_op jit(solution)/shard_map/psum | solution.py:30
  830.5 0.6 multiply_reduce_fusion
  831.2 29.3 %psum.15 = f32[]{:T(128)} all-reduce(f32[]{:T(128)} %multiply_reduce_fusion), channel_id=1, replica_groups=mesh['row'=8,'col'=16] {'row'}, use_global_device_ids=true, to_apply=%region_2.0 | all-reduce | flops 1 | bytes 8 | tf_op jit(solution)/shard_map/psum | solution.py:31
  861.2 0.6 broadcast_multiply_fusion.1
Async XLA Ops:
  0.6 748.2 %copy-start = (bf16[2,192,3072]{2,1,0:T(8,128)(2,1)S(1)}, bf16[2,192,3072]{2,1,0:T(8,128)(2,1)}, u32[]{:S(2)}) copy-start(bf16[2,192,3072]{2,1,0:T(8,128)(2,1)} %param.4) | copy-start | bytes 7077892
  14.4 7.8 copy-start.1
  14.4 709.0 %all-to-all-start = ((bf16[16,2,192,3072]{3,2,1,0:T(8,128)(2,1)}), bf16[16,2,192,3072]{3,2,1,0:T(8,128)(2,1)}, u32[]{:S(2)}, u32[]{:S(2)}) async-start(bf16[16,2,192,3072]{3,2,1,0:T(8,128)(2,1)} %stack.2), calls=%async_computation | async-start | bytes 75497472 | tf_op jit(solution)/shard_map/all_to_all | solution.py:21
